TPU v7x, 128 devices: a whole 4x4x4 slice. The times are simulated.
128 devices in a mesh: batch: 4 (over z), head: 2 (over core), seq: 16 (over x, y).
Axes of the slice: x: 4, y: 4, z: 4, core: 2. Of those that a mesh axis runs over, the one named last changes fastest.
Arguments:
- hidden: float32 [32768, 8192], P(('batch', 'seq')), parts along dimension 0, may hold values from -6 to 6
- row_scale: float32 [32768], P(('batch', 'seq')), parts along dimension 0, may hold values from 0.25 to 4
- key_value_weight: float32 [8192, 8, 256], P('seq', 'head'), may hold values from -0.0625 to 0.0625
- outlier: int32 [512, 8], P(('batch', 'seq'), 'head'), parts along dimension 0, may hold values 0 or 1
- sketch_sign_flags: int32 [8, 2, 128, 64], P('head'), may hold values from 0 to 1
Outputs:
- left: bfloat16 [8, 32768, 128], P('head', ('batch', 'seq')), parts along dimension 1
- right: float32 [32, 128, 128], P(('batch', 'head')), parts along dimension 0
There are 4 independent parts, one for each index of `batch`. A program takes and returns all parts, laid end to end along the dimension named above; an argument that names none is the same for every part. Nothing has to cross between parts.
All inputs are finite; a program needn't handle non-finite values. No bound on the sum of `outlier` on one device may be relied on, other than what follows from the above.
Results may differ from a plain program's by a relative error of at most 0.0015.
Values sent between devices are 32-bit elements; how exact they have to be, the bound alone decides.
No kernel may reach another device: no remote copies, remote signals or barrier semaphores. Data moves between devices by JAX's collectives and lax.ppermute only.
A program may use at most 192 MiB of HBM per device.

v0:
```python
import math
import jax
import jax.numpy as jnp
from jax import lax
from jax.sharding import PartitionSpec as P

ITERS = 2
complete_cycle = 2.0 * math.pi


def shards(hidden, row_scale, key_value_weight, outlier, sketch_sign_flags):
    tok_rows = hidden.shape[0]
    head_count = key_value_weight.shape[1]
    kv_cols = key_value_weight.shape[2]
    head_dim = kv_cols // 2
    rank_cols = sketch_sign_flags.shape[3]
    group_count = outlier.shape[0]
    highest = lax.Precision.HIGHEST
    weight_piece = lax.all_gather(key_value_weight, "seq", axis=0, tiled=True)
    flat_piece = weight_piece.reshape(weight_piece.shape[0], head_count * kv_cols)
    projected_key_value = jnp.dot(hidden, flat_piece, precision=highest)
    projected_key_value = projected_key_value * row_scale[:, None]
    grouped_rows = projected_key_value.reshape(
        group_count, tok_rows // group_count, head_count, kv_cols
    )
    quantization_spacing = jnp.max(jnp.abs(grouped_rows), axis=1, keepdims=True) / 7.0 + 1e-06
    retain_mask = (1 - outlier).astype(jnp.float32)[:, None, :, None]
    residual_error = (
        retain_mask * jnp.sin(complete_cycle * grouped_rows / quantization_spacing)
    ).reshape(tok_rows, head_count, 2, head_dim)
    sign_matrix = (2 * sketch_sign_flags - 1).astype(jnp.float32)
    sketch = jnp.einsum("thec,heck->thek", residual_error, sign_matrix, precision=highest)
    for iteration in range(ITERS):
        local_gram = jnp.einsum("thek,theq->hekq", sketch, sketch, precision=highest)
        gram_matrix = lax.psum(local_gram, "seq")
        lower_factor = jnp.linalg.cholesky(gram_matrix)
        identity = jnp.broadcast_to(jnp.eye(rank_cols, dtype=gram_matrix.dtype), gram_matrix.shape)
        inverse_factor = jax.scipy.linalg.solve_triangular(lower_factor, identity, lower=True)
        basis_matrix = jnp.einsum("thek,heqk->theq", sketch, inverse_factor, precision=highest)
        local_coef = jnp.einsum("thec,theq->hecq", residual_error, basis_matrix, precision=highest)
        coefficient_rows = lax.psum(local_coef, "seq")
        if iteration + 1 < ITERS:
            sketch = jnp.einsum(
                "thec,hecq->theq", residual_error, coefficient_rows, precision=highest
            )
    root_length = math.sqrt(tok_rows * lax.axis_size("seq"))
    left = (
        (root_length * basis_matrix)
        .transpose(1, 0, 2, 3)
        .reshape(head_count, tok_rows, 2 * rank_cols)
        .astype(jnp.bfloat16)
    )
    right = (
        (coefficient_rows / root_length)
        .transpose(0, 2, 1, 3)
        .reshape(head_count, head_dim, 2 * rank_cols)
    )
    return (left, right)


def solution(mesh):
    return jax.shard_map(
        shards,
        mesh=mesh,
        in_specs=(
            P(("batch", "seq"), None),
            P(("batch", "seq")),
            P("seq", "head", None),
            P(("batch", "seq"), "head"),
            P("head", None, None, None),
        ),
        out_specs=(P("head", ("batch", "seq"), None), P(("batch", "head"), None, None)),
        check_vma=False,
    )
```

profile of v0, /device:TPU:0, one launch (start us, length us, event | category | flops | bytes accessed | tf_op | source)
XLA Modules:
  0.0 858.8 jit_solution(14637617141155702260)
XLA Ops:
  7.2 0.0 copy-start.2
  7.2 0.0 all-gather.2.cloned.1.call-start
  7.2 0.7 all-gather.2.cloned.1.call-update
  7.9 0.0 all-reduce.5.cloned.1.call-start
  8.0 0.0 copy-done.2
  8.0 0.1 mul.45
  8.0 0.1 mul.46
  8.1 201.4 %all-gather.2.cloned.1.call-done = f32[8192,4,256]{2,1,0:T(4,128)} async-done(((f32[512,4,256]{2,1,0:T(4,128)}), f32[8192,4,256]{2,1,0:T(4,128)}) %all-gather.2.cloned.1.call-update) | async-done | bytes 33554448 | tf_op jit(solution)/shard_map/all_gather | solution.py:19
  209.6 0.0 copy-start.3
  209.6 27.5 %copy.108 = f32[1024,8,4,256]{3,1,2,0:T(8,128)} copy(f32[1024,8,4,256]{3,2,1,0:T(4,128)} %bitcast.58) | data formatting | bytes 67108864
  237.1 0.0 copy-done.3
  237.1 60.5 %multiply_abs_fusion = (f32[512,1024]{1,0:T(8,128)}, f32[512,1024]{1,0:T(8,128)}) fusion(f32[512]{0:T(512)S(1)} %copy-done.3, f32[512,8192]{1,0:T(8,128)} %param.8, f32[8192,1024]{1,0:T(8,128)} %bitcast.59), kind=kOutput, calls=%fused_computation.3 | convolution fusion | flops 51541180416 | bytes 54528000 | tf_op jit(solution)/shard_map/dot_general | solution.py:21
  297.6 2.2 abs.7
  299.8 0.3 reduce_max.9
  300.1 0.2 div.31
  300.3 2.1 div.32
  302.4 1.9 copy.86
  304.4 1.8 copy.88
  306.2 0.0 copy-start.1
  306.2 8.9 %fusion.1 = f32[512,4,2,128]{3,0,2,1:T(8,128)S(1)} fusion(f32[512,4,2,128]{3,0,2,1:T(8,128)} %copy.88, f32[512,4,2,128]{3,2,0,1:T(2,128)} %div.32, f32[512,4]{0,1:T(4,128)S(1)} %mul.46), kind=kLoop, calls=%fused_computation.2 | loop fusion | flops 1048576 | bytes 6299648 | tf_op jit(solution)/shard_map/mul | solution.py:29
  315.1 0.0 copy-done.1
  315.1 2.4 convolution_bitcast_fusion.1
  317.5 1.8 fusion.21
  319.3 0.0 all-reduce.5.cloned.1.call-update
  319.3 0.0 all-reduce.7.cloned.1.call-start
  319.4 83.9 %all-reduce.5.cloned.1.call-done = f32[4,2,64,64]{2,3,1,0:T(8,128)} async-done(((f32[4,2,64,64]{2,3,1,0:T(8,128)}), f32[4,2,64,64]{2,3,1,0:T(8,128)}) %all-reduce.5.cloned.1.call-update) | async-done | bytes 131088 | tf_op jit(solution)/shard_map/psum | solution.py:35
  403.3 1.1 copy.91
  404.3 1.7 fusion.9
  406.0 47.6 %custom-call.8 = f32[4,2,64,64]{3,2,1,0:T(8,128)S(1)} custom-call(f32[4,2,64,64]{3,2,1,0:T(8,128)} %fusion.9), custom_call_target="Cholesky" | custom-call | tf_op jit(solution)/shard_map/jit(cholesky)/cholesky | solution.py:36
  453.7 0.1 compare_reduce_fusion.1
  453.8 0.8 select_bitcast_fusion.1
  454.7 40.0 %custom-call.9 = f32[4,2,1,64,64]{3,4,2,1,0:T(8,128)S(1)} custom-call(f32[4,2,1,64,64]{4,3,2,1,0:T(8,128)} %select_bitcast_fusion.1), custom_call_target="InvertDiagBlocksLowerTriangular" | custom-call | tf_op jit(solution)/shard_map/jit(_solve_triangular)/vmap(vmap())/triangular_solve | solution.py:38
  494.7 0.6 fusion.7
  495.3 1.0 convolution_bitcast_fusion.2
  496.3 2.2 fusion.22
  498.5 0.0 all-reduce.7.cloned.1.call-update
  498.6 0.0 all-reduce.9.cloned.1.call-start
  498.6 83.5 %all-reduce.7.cloned.1.call-done = f32[4,2,128,64]{2,3,1,0:T(8,128)} async-done(((f32[4,2,128,64]{2,3,1,0:T(8,128)}), f32[4,2,128,64]{2,3,1,0:T(8,128)}) %all-reduce.7.cloned.1.call-update) | async-done | bytes 262160 | tf_op jit(solution)/shard_map/psum | solution.py:41
  582.1 3.3 convolution_bitcast_fusion
  585.4 1.8 fusion.23
  587.2 0.0 all-reduce.9.cloned.1.call-update
  587.2 0.0 all-reduce.11.cloned.1.call-start
  587.3 83.6 %all-reduce.9.cloned.1.call-done = f32[4,2,64,64]{2,3,1,0:T(8,128)} async-done(((f32[4,2,64,64]{2,3,1,0:T(8,128)}), f32[4,2,64,64]{2,3,1,0:T(8,128)}) %all-reduce.9.cloned.1.call-update) | async-done | bytes 131088 | tf_op jit(solution)/shard_map/psum | solution.py:35
  670.8 1.1 copy.96
  671.9 1.7 fusion.6
  673.6 47.6 %custom-call.10 = f32[4,2,64,64]{3,2,1,0:T(8,128)S(1)} custom-call(f32[4,2,64,64]{3,2,1,0:T(8,128)} %fusion.6), custom_call_target="Cholesky" | custom-call | tf_op jit(solution)/shard_map/jit(cholesky)/cholesky | solution.py:36
  721.3 0.1 compare_reduce_fusion
  721.4 0.8 select_bitcast_fusion
  722.2 40.0 %custom-call.11 = f32[4,2,1,64,64]{3,4,2,1,0:T(8,128)S(1)} custom-call(f32[4,2,1,64,64]{4,3,2,1,0:T(8,128)} %select_bitcast_fusion), custom_call_target="InvertDiagBlocksLowerTriangular" | custom-call | tf_op jit(solution)/shard_map/jit(_solve_triangular)/vmap(vmap())/triangular_solve | solution.py:38
  762.3 0.6 fusion.4
  762.9 1.8 multiply_convert_fusion
  764.7 0.0 copy-start
  764.7 2.2 fusion.2
  766.9 0.0 all-reduce.11.cloned.1.call-update
  766.9 0.0 copy-done
  766.9 1.0 copy.100
  767.9 82.5 %all-reduce.11.cloned.1.call-done = f32[4,2,128,64]{2,3,1,0:T(8,128)} async-done(((f32[4,2,128,64]{2,3,1,0:T(8,128)}), f32[4,2,128,64]{2,3,1,0:T(8,128)}) %all-reduce.11.cloned.1.call-update) | async-done | bytes 262160 | tf_op jit(solution)/shard_map/psum | solution.py:41
  850.5 1.0 broadcast_multiply_fusion
  851.4 0.8 copy.101
  (7 shorter events, 0.1 us)
Async XLA Ops:
  7.2 0.8 copy-start.2
  7.2 202.4 %all-gather.2.cloned.1.call-start = ((), (), s32[]{:S(2)}) async-start(), calls=%async_computation | async-start | bytes 35651584 | tf_op jit(solution)/shard_map/all_gather | solution.py:19
  7.9 395.4 %all-reduce.5.cloned.1.call-start = ((), (), s32[]{:S(2)}) async-start(), calls=%async_computation.1 | async-start | bytes 524288 | tf_op jit(solution)/shard_map/psum | solution.py:35
  209.6 27.5 %copy-start.3 = (f32[512]{0:T(512)S(1)}, f32[512]{0:T(512)}, u32[]{:S(2)}) copy-start(f32[512]{0:T(512)} %param.9) | copy-start | bytes 6148
  306.2 8.9 %copy-start.1 = (s32[4,2,128,64]{2,3,1,0:T(8,128)S(1)}, s32[4,2,128,64]{2,3,1,0:T(8,128)}, u32[]{:S(2)}) copy-start(s32[4,2,128,64]{2,3,1,0:T(8,128)} %param.12) | copy-start | bytes 786436
  319.3 262.8 %all-reduce.7.cloned.1.call-start = ((), (), s32[]{:S(2)}) async-start(), calls=%async_computation.2 | async-start | bytes 524288 | tf_op jit(solution)/shard_map/psum | solution.py:41
  498.6 172.3 %all-reduce.9.cloned.1.call-start = ((), (), s32[]{:S(2)}) async-start(), calls=%async_computation.3 | async-start | bytes 524288 | tf_op jit(solution)/shard_map/psum | solution.py:35
  587.2 263.2 %all-reduce.11.cloned.1.call-start = ((), (), s32[]{:S(2)}) async-start(), calls=%async_computation.4 | async-start | bytes 524288 | tf_op jit(solution)/shard_map/psum | solution.py:41
  764.7 2.3 copy-start
Sparse Core Ops, SparseCore 0:
  10.1 199.3 all-gather.1
  319.4 83.7 all-reduce.4
  498.7 83.3 all-reduce.6
  587.3 83.4 all-reduce.8
  767.1 83.3 all-reduce.10
where the time goes:
time: 860 us; the launch traced here: 859 us
  waiting for transfers between devices  536 us (62%)
  other arithmetic  191 us (22%)
  matrix products  78.2 us (9%)
  local copies, waits for them, and re-layouts  39.9 us (5%)
  between operations  14 us (2%)
    all_gather x1, waiting for transfers between devices, shards(): weight_piece = lax.all_gather(key_value_weight, 'seq', axis=0, tiled=True)  201 us
    psum x2, waiting for transfers between devices, shards(): gram_matrix = lax.psum(local_gram, 'seq')  167 us
    psum x2, waiting for transfers between devices, shards(): coefficient_rows = lax.psum(local_coef, 'seq')  166 us
    another operation x7, other arithmetic, shards(): lower_factor = jnp.linalg.cholesky(gram_matrix)  95.6 us
    another operation x5, other arithmetic, shards(): jax.scipy.linalg.solve_triangular(lower_factor, identity, lower=True)  81.7 us
    dot_general x1, matrix products, shards(): projected_key_value = jnp.dot(hidden, flat_piece, precision=highest)  60.5 us
    unnamed x11, local copies, waits for them, and re-layouts  29.4 us
  transfers between devices with their start and end apart: 5, of which 5 were waited for; matrix products, arithmetic and copies ran while one was open for 0% of the time, Pallas kernels for 0%

commit v1 on v0

--- a/solution.py
+++ b/solution.py
@@ -38,7 +38,11 @@
         inverse_factor = jax.scipy.linalg.solve_triangular(lower_factor, identity, lower=True)
         basis_matrix = jnp.einsum("thek,heqk->theq", sketch, inverse_factor, precision=highest)
         local_coef = jnp.einsum("thec,theq->hecq", residual_error, basis_matrix, precision=highest)
-        coefficient_rows = lax.psum(local_coef, "seq")
+        coefficient_rows = local_coef
+        for hop in (1, 2, 4, 8):
+            coefficient_rows = coefficient_rows + lax.ppermute(
+                coefficient_rows, "seq", [(dev, dev ^ hop) for dev in range(16)]
+            )
         if iteration + 1 < ITERS:
             sketch = jnp.einsum(
                 "thec,hecq->theq", residual_error, coefficient_rows, precision=highest

time: 860 us -> 752 us (0.87)
  waiting for transfers between devices: 536 us -> 422 us
  starting transfers between devices: 0.2 us -> 9.17 us
    psum x2 -> x0, waiting for transfers between devices: 166 us -> none  [shards(): coefficient_rows = lax.psum(local_coef, 'seq')]
    ppermute x0 -> x8, waiting for transfers between devices: none -> 52.5 us  [shards(): lax.ppermute(coefficient_rows, 'seq', [(dev, dev ^ hop) for dev in range(...]
    ppermute x0 -> x8, starting transfers between devices: none -> 9.05 us  [shards(): lax.ppermute(coefficient_rows, 'seq', [(dev, dev ^ hop) for dev in range(...]
  transfers between devices with their start and end apart: 5 -> 11, of which waited for: 5 -> 11; matrix products, arithmetic and copies ran while one was open for 0% -> 0% of each run, Pallas kernels for 0% -> 0%
where the time goes in v1:
time: 752 us; the launch traced here: 751 us
  waiting for transfers between devices  422 us (56%)
  other arithmetic  190 us (25%)
  matrix products  76 us (10%)
  local copies, waits for them, and re-layouts  39.9 us (5%)
  between operations  14 us (2%)
  starting transfers between devices  9.17 us (1%)
    all_gather x1, waiting for transfers between devices, shards(): weight_piece = lax.all_gather(key_value_weight, 'seq', axis=0, tiled=True)  201 us
    psum x2, waiting for transfers between devices, shards(): gram_matrix = lax.psum(local_gram, 'seq')  167 us
    another operation x7, other arithmetic, shards(): lower_factor = jnp.linalg.cholesky(gram_matrix)  95.6 us
    another operation x5, other arithmetic, shards(): jax.scipy.linalg.solve_triangular(lower_factor, identity, lower=True)  81.7 us
    dot_general x1, matrix products, shards(): projected_key_value = jnp.dot(hidden, flat_piece, precision=highest)  60.5 us
    ppermute x8, waiting for transfers between devices, shards(): lax.ppermute(coefficient_rows, 'seq', [(dev, dev ^ hop) for dev in range(...  52.5 us
    unnamed x11, local copies, waits for them, and re-layouts  29.4 us
  transfers between devices with their start and end apart: 11, of which 11 were waited for; matrix products, arithmetic and copies ran while one was open for 0% of the time, Pallas kernels for 0%

profile of v1, /device:TPU:0, one launch (start us, length us, event | category | flops | bytes accessed | tf_op | source)
XLA Modules:
  0.0 751.1 jit_solution(3472407862824462253)
XLA Ops:
  7.2 0.0 copy-start.2
  7.2 0.0 all-gather.2.cloned.1.call-start
  7.2 0.7 all-gather.2.cloned.1.call-update
  7.9 0.0 all-reduce.3.cloned.1.call-start
  8.0 0.0 copy-done.2
  8.0 0.1 mul.45
  8.0 0.1 mul.46
  8.1 201.4 %all-gather.2.cloned.1.call-done = f32[8192,4,256]{2,1,0:T(4,128)} async-done(((f32[512,4,256]{2,1,0:T(4,128)}), f32[8192,4,256]{2,1,0:T(4,128)}) %all-gather.2.cloned.1.call-update) | async-done | bytes 33554448 | tf_op jit(solution)/shard_map/all_gather | solution.py:19
  209.6 27.5 %copy.109 = f32[1024,8,4,256]{3,1,2,0:T(8,128)} copy(f32[1024,8,4,256]{3,2,1,0:T(4,128)} %bitcast.57) | data formatting | bytes 67108864
  237.1 0.0 copy-done.3
  237.1 60.5 %multiply_abs_fusion = (f32[512,1024]{1,0:T(8,128)}, f32[512,1024]{1,0:T(8,128)}) fusion(f32[512]{0:T(512)S(1)} %copy-done.3, f32[512,8192]{1,0:T(8,128)} %param.8, f32[8192,1024]{1,0:T(8,128)} %bitcast.58), kind=kOutput, calls=%fused_computation.3 | convolution fusion | flops 51541180416 | bytes 54528000 | tf_op jit(solution)/shard_map/dot_general | solution.py:21
  297.6 2.2 abs.7
  299.8 0.3 reduce_max.9
  300.1 0.2 div.31
  300.3 2.1 div.32
  302.4 1.9 copy.87
  304.4 1.8 copy.89
  306.2 8.9 %fusion.1 = f32[512,4,2,128]{3,0,2,1:T(8,128)S(1)} fusion(f32[512,4,2,128]{3,0,2,1:T(8,128)} %copy.89, f32[512,4,2,128]{3,2,0,1:T(2,128)} %div.32, f32[512,4]{0,1:T(4,128)S(1)} %mul.46), kind=kLoop, calls=%fused_computation.2 | loop fusion | flops 1048576 | bytes 6299648 | tf_op jit(solution)/shard_map/mul | solution.py:29
  315.1 0.0 copy-done.1
  315.1 2.4 convolution_bitcast_fusion.1
  317.5 1.8 fusion.22
  319.2 0.0 all-reduce.3.cloned.1.call-update
  319.3 0.0 all-reduce.5.cloned.1.call-start
  319.4 83.8 %all-reduce.3.cloned.1.call-done = f32[4,2,64,64]{2,3,1,0:T(8,128)} async-done(((f32[4,2,64,64]{2,3,1,0:T(8,128)}), f32[4,2,64,64]{2,3,1,0:T(8,128)}) %all-reduce.3.cloned.1.call-update) | async-done | bytes 131088 | tf_op jit(solution)/shard_map/psum | solution.py:35
  403.2 1.1 copy.92
  404.3 1.7 fusion.9
  406.0 47.6 %custom-call.8 = f32[4,2,64,64]{3,2,1,0:T(8,128)S(1)} custom-call(f32[4,2,64,64]{3,2,1,0:T(8,128)} %fusion.9), custom_call_target="Cholesky" | custom-call | tf_op jit(solution)/shard_map/jit(cholesky)/cholesky | solution.py:36
  453.6 0.1 compare_reduce_fusion.1
  453.8 0.8 select_bitcast_fusion.1
  454.6 40.0 %custom-call.9 = f32[4,2,1,64,64]{3,4,2,1,0:T(8,128)S(1)} custom-call(f32[4,2,1,64,64]{4,3,2,1,0:T(8,128)} %select_bitcast_fusion.1), custom_call_target="InvertDiagBlocksLowerTriangular" | custom-call | tf_op jit(solution)/shard_map/jit(_solve_triangular)/vmap(vmap())/triangular_solve | solution.py:38
  494.7 0.6 fusion.7
  495.3 1.0 convolution_bitcast_fusion.2
  496.2 1.6 fusion.23
  497.9 1.2 collective-permute-start
  499.1 5.6 collective-permute-done
  504.8 1.6 collective-permute-start.1
  506.4 6.4 collective-permute-done.1
  512.8 0.9 collective-permute-start.2
  513.7 7.4 collective-permute-done.2
  521.1 1.0 collective-permute-start.3
  522.0 7.2 collective-permute-done.3
  529.3 2.4 convolution_bitcast_fusion
  531.6 1.8 fusion.24
  533.4 0.0 all-reduce.5.cloned.1.call-update
  533.4 83.4 %all-reduce.5.cloned.1.call-done = f32[4,2,64,64]{2,3,1,0:T(8,128)} async-done(((f32[4,2,64,64]{2,3,1,0:T(8,128)}), f32[4,2,64,64]{2,3,1,0:T(8,128)}) %all-reduce.5.cloned.1.call-update) | async-done | bytes 131088 | tf_op jit(solution)/shard_map/psum | solution.py:35
  616.8 1.1 copy.97
  617.9 1.7 fusion.6
  619.6 47.6 %custom-call.10 = f32[4,2,64,64]{3,2,1,0:T(8,128)S(1)} custom-call(f32[4,2,64,64]{3,2,1,0:T(8,128)} %fusion.6), custom_call_target="Cholesky" | custom-call | tf_op jit(solution)/shard_map/jit(cholesky)/cholesky | solution.py:36
  667.2 0.1 compare_reduce_fusion
  667.4 0.8 select_bitcast_fusion
  668.2 40.0 %custom-call.11 = f32[4,2,1,64,64]{3,4,2,1,0:T(8,128)S(1)} custom-call(f32[4,2,1,64,64]{4,3,2,1,0:T(8,128)} %select_bitcast_fusion), custom_call_target="InvertDiagBlocksLowerTriangular" | custom-call | tf_op jit(solution)/shard_map/jit(_solve_triangular)/vmap(vmap())/triangular_solve | solution.py:38
  708.3 0.6 fusion.4
  708.9 1.8 multiply_convert_fusion
  710.6 1.6 fusion.2
  712.3 1.2 collective-permute-start.4
  713.5 5.7 collective-permute-done.4
  719.2 1.6 collective-permute-start.5
  720.8 6.4 collective-permute-done.5
  727.2 0.9 collective-permute-start.6
  728.1 7.6 %collective-permute-done.6 = f32[4,2,128,64]{2,3,1,0:T(8,128)S(1)} collective-permute-done((f32[4,2,128,64]{2,3,1,0:T(8,128)S(1)}, f32[4,2,128,64]{2,3,1,0:T(8,128)S(1)}, u32[]{:S(2)}, u32[]{:S(2)}) %collective-permute-start.6) | collective-permute-done | bytes 262176 | tf_op jit(solution)/shard_map/ppermute | solution.py:43
  735.7 0.7 collective-permute-start.7
  736.5 1.0 copy.101
  737.5 6.2 collective-permute-done.7
  743.7 0.8 copy.102
  (18 shorter events, 0.4 us)
Async XLA Ops:
  7.2 0.8 copy-start.2
  7.2 202.4 %all-gather.2.cloned.1.call-start = ((), (), s32[]{:S(2)}) async-start(), calls=%async_computation | async-start | bytes 35651584 | tf_op jit(solution)/shard_map/all_gather | solution.py:19
  7.9 395.3 %all-reduce.3.cloned.1.call-start = ((), (), s32[]{:S(2)}) async-start(), calls=%async_computation.1 | async-start | bytes 524288 | tf_op jit(solution)/shard_map/psum | solution.py:35
  209.6 27.6 %copy-start.3 = (f32[512]{0:T(512)S(1)}, f32[512]{0:T(512)}, u32[]{:S(2)}) copy-start(f32[512]{0:T(512)} %param.9) | copy-start | bytes 6148
  306.2 8.9 %copy-start.1 = (s32[4,2,128,64]{2,3,1,0:T(8,128)S(1)}, s32[4,2,128,64]{2,3,1,0:T(8,128)}, u32[]{:S(2)}) copy-start(s32[4,2,128,64]{2,3,1,0:T(8,128)} %param.12) | copy-start | bytes 786436
  319.3 297.5 %all-reduce.5.cloned.1.call-start = ((), (), s32[]{:S(2)}) async-start(), calls=%async_computation.2 | async-start | bytes 524288 | tf_op jit(solution)/shard_map/psum | solution.py:35
  497.9 6.9 collective-permute-start
  504.8 8.0 %collective-permute-start.1 = (f32[4,2,128,64]{2,3,1,0:T(8,128)S(1)}, f32[4,2,128,64]{2,3,1,0:T(8,128)S(1)}, u32[]{:S(2)}, u32[]{:S(2)}) collective-permute-start(f32[4,2,128,64]{2,3,1,0:T(8,128)S(1)} %add.51), channel_id=1, source_target_pairs={{0,2},{1,3},{2,0},{3,1},{4,6},{5,7},{6,4},{7,5},{8,10},{9,11},{10,... | collective-permute-start | bytes 786440 | tf_op jit(solution)/shard_map/ppermute | solution.py:43
  512.8 8.3 %collective-permute-start.2 = (f32[4,2,128,64]{2,3,1,0:T(8,128)S(1)}, f32[4,2,128,64]{2,3,1,0:T(8,128)S(1)}, u32[]{:S(2)}, u32[]{:S(2)}) collective-permute-start(f32[4,2,128,64]{2,3,1,0:T(8,128)S(1)} %add.52), channel_id=1, source_target_pairs={{0,4},{1,5},{2,6},{3,7},{4,0},{5,1},{6,2},{7,3},{8,12},{9,13},{10,... | collective-permute-start | bytes 786440 | tf_op jit(solution)/shard_map/ppermute | solution.py:43
  521.1 8.2 %collective-permute-start.3 = (f32[4,2,128,64]{2,3,1,0:T(8,128)S(1)}, f32[4,2,128,64]{2,3,1,0:T(8,128)S(1)}, u32[]{:S(2)}, u32[]{:S(2)}) collective-permute-start(f32[4,2,128,64]{2,3,1,0:T(8,128)S(1)} %add.53), channel_id=1, source_target_pairs={{0,8},{1,9},{2,10},{3,11},{4,12},{5,13},{6,14},{7,15},{8,0},{9,1},... | collective-permute-start | bytes 786440 | tf_op jit(solution)/shard_map/ppermute | solution.py:43
  710.6 25.8 %copy-start = (bf16[4,2,64,512]{3,2,1,0:T(8,128)(2,1)S(1)}, bf16[4,2,64,512]{3,2,1,0:T(8,128)(2,1)}, u32[]{:S(2)}) copy-start(bf16[4,2,64,512]{3,2,1,0:T(8,128)(2,1)} %get-tuple-element.20) | copy-start | bytes 1572868
  712.3 6.9 collective-permute-start.4
  719.2 8.0 %collective-permute-start.5 = (f32[4,2,128,64]{2,3,1,0:T(8,128)S(1)}, f32[4,2,128,64]{2,3,1,0:T(8,128)S(1)}, u32[]{:S(2)}, u32[]{:S(2)}) collective-permute-start(f32[4,2,128,64]{2,3,1,0:T(8,128)S(1)} %add.55), channel_id=1, source_target_pairs={{0,2},{1,3},{2,0},{3,1},{4,6},{5,7},{6,4},{7,5},{8,10},{9,11},{10,... | collective-permute-start | bytes 786440 | tf_op jit(solution)/shard_map/ppermute | solution.py:43
  727.2 8.5 %collective-permute-start.6 = (f32[4,2,128,64]{2,3,1,0:T(8,128)S(1)}, f32[4,2,128,64]{2,3,1,0:T(8,128)S(1)}, u32[]{:S(2)}, u32[]{:S(2)}) collective-permute-start(f32[4,2,128,64]{2,3,1,0:T(8,128)S(1)} %add.56), channel_id=1, source_target_pairs={{0,4},{1,5},{2,6},{3,7},{4,0},{5,1},{6,2},{7,3},{8,12},{9,13},{10,... | collective-permute-start | bytes 786440 | tf_op jit(solution)/shard_map/ppermute | solution.py:43
  735.7 8.0 %collective-permute-start.7 = (f32[4,2,128,64]{2,3,1,0:T(8,128)S(1)}, f32[4,2,128,64]{2,3,1,0:T(8,128)S(1)}, u32[]{:S(2)}, u32[]{:S(2)}) collective-permute-start(f32[4,2,128,64]{2,3,1,0:T(8,128)S(1)} %add.57), channel_id=1, source_target_pairs={{0,8},{1,9},{2,10},{3,11},{4,12},{5,13},{6,14},{7,15},{8,0},{9,1},... | collective-permute-start | bytes 786440 | tf_op jit(solution)/shard_map/ppermute | solution.py:43
Sparse Core Ops, SparseCore 0:
  10.1 199.3 all-gather.1
  319.4 83.7 all-reduce.2
  533.5 83.2 all-reduce.4
